TPU v7x, 512 devices: a whole 4x4x16 slice. The times are simulated.
512 devices in a mesh: dp: 128 (over z, x, core), layer: 4 (over y).
Axes of the slice: x: 4, y: 4, z: 16, core: 2. Of those that a mesh axis runs over, the one named last changes fastest.
Arguments:
- micro_grads: bfloat16 [4, 128, 256, 2048], P('layer', 'dp')
- master: float32 [4, 384, 2, 2048], P('layer', 'dp'), may hold values from -6 to 6
- moment_one: float32 [4, 384, 2, 2048], P('layer', 'dp'), may hold values from -4 to 4
- moment_two: float32 [4, 384, 2, 2048], P('layer', 'dp'), may hold values from 0.01 to 1
- owner: int32 [4, 128], P('layer'), may hold values from 0 to 127, as said below
- slot: int32 [4, 128], P('layer'), may hold values from 0 to 2, as said below
Outputs:
- new_master: float32 [4, 384, 2, 2048], P('layer', 'dp')
- new_moment_one: float32 [4, 384, 2, 2048], P('layer', 'dp')
- new_moment_two: float32 [4, 384, 2, 2048], P('layer', 'dp')
- weights: bfloat16 [4, 256, 2048], P('layer')
- grad_rms: float32 [], replicated
Inputs may be any that keep to these rules, and one draw needn't show every extreme that they name: In every layer no owner holds more than 3 blocks, and some owner holds exactly 3. The pairs (owner, slot) of one layer are all different.
All inputs are finite; a program needn't handle non-finite values.
Results may differ from a plain program's by a relative error of at most 0.0004.
Values may be sent and summed in bfloat16 or wider, within the bound.
No kernel may reach another device: no remote copies, remote signals or barrier semaphores. Data moves between devices by JAX's collectives and lax.ppermute only.
A program may use at most 64 MiB of HBM per device.

v0:
```python
import jax
import jax.numpy as jnp
from jax import lax
from jax.sharding import PartitionSpec as P

beta_one = 0.9
beta_two = 0.95
learn_rate = 0.0003
decay_rate = 0.1
adam_eps = 1e-08
step_number = 100.0


def adamw(param, first, second, grad):
    first_new = beta_one * first + (1.0 - beta_one) * grad
    second_new = beta_two * second + (1.0 - beta_two) * grad * grad
    corr_one = 1.0 - beta_one**step_number
    corr_two = 1.0 - beta_two**step_number
    update = (
        first_new / corr_one / (jnp.sqrt(second_new / corr_two) + adam_eps) + decay_rate * param
    )
    return (param - learn_rate * update, first_new, second_new)


def shards(micro_grads, master, moment_one, moment_two, owner, slot):
    my_index = lax.axis_index("dp")
    row_count = micro_grads.shape[2]
    feature_count = micro_grads.shape[3]
    capacity = master.shape[1]
    slab_rows = master.shape[2]
    block_count = owner.shape[1]
    summed = micro_grads[0, 0].astype(jnp.float32)
    flat_grad = summed.reshape(-1, 128)
    grad_share = lax.psum_scatter(flat_grad, "dp", scatter_dimension=0, tiled=True)
    reduced = lax.all_gather(grad_share, "dp", axis=0, tiled=True).reshape(row_count, feature_count)
    squares = lax.psum(jnp.sum(grad_share * grad_share), ("dp", "layer"))
    element_total = lax.axis_size("layer") * row_count * feature_count
    grad_rms = jnp.sqrt(squares / element_total + 1e-06)
    clip_factor = jnp.minimum(1.0, 1.0 / grad_rms)
    owners = owner[0]
    slots_of = slot[0]
    slot_ids = jnp.arange(capacity, dtype=jnp.int32)
    matches = (owners[None, :] == my_index) & (slots_of[None, :] == slot_ids[:, None])
    filled = jnp.any(matches, axis=1)
    block_of_slot = jnp.sum(
        jnp.where(matches, jnp.arange(block_count, dtype=jnp.int32)[None, :], 0), axis=1
    )
    blocks_grad = reduced.reshape(block_count, slab_rows, feature_count)
    grad_slots = jnp.take(blocks_grad, block_of_slot, axis=0) * clip_factor
    param, first, second = adamw(master[0], moment_one[0], moment_two[0], grad_slots)
    keep = filled[:, None, None]
    new_master = jnp.where(keep, param, master[0])
    new_first = jnp.where(keep, first, moment_one[0])
    new_second = jnp.where(keep, second, moment_two[0])
    slot_weights = param.astype(jnp.bfloat16)
    mine = owners == my_index
    block_weights = jnp.take(slot_weights, slots_of, axis=0)
    placed = jnp.where(mine[:, None, None], block_weights.astype(jnp.float32), 0.0).reshape(-1, 128)
    weight_share = lax.psum_scatter(placed, "dp", scatter_dimension=0, tiled=True).astype(
        jnp.bfloat16
    )
    weights = lax.all_gather(weight_share, "dp", axis=0, tiled=True).reshape(
        row_count, feature_count
    )
    return (new_master[None], new_first[None], new_second[None], weights[None], grad_rms)


def solution(mesh):
    in_specs = (
        P("layer", "dp", None, None),
        P("layer", "dp", None, None),
        P("layer", "dp", None, None),
        P("layer", "dp", None, None),
        P("layer", None),
        P("layer", None),
    )
    out_specs = (
        P("layer", "dp", None, None),
        P("layer", "dp", None, None),
        P("layer", "dp", None, None),
        P("layer", None, None),
        P(),
    )
    return jax.shard_map(shards, mesh=mesh, in_specs=in_specs, out_specs=out_specs, check_vma=False)
```

profile of v0, /device:TPU:1, one launch (start us, length us, event | category | flops | bytes accessed | tf_op | source)
XLA Modules:
  0.0 830.3 jit_solution(17510532060689569105)
XLA Ops:
  7.2 0.0 copy-start.4
  7.2 0.0 copy-start.3
  7.2 0.0 reduce-scatter.3.cloned.1.call-start
  7.2 2.6 reshape.111
  9.8 0.0 reduce-scatter.3.cloned.1.call-update
  9.9 0.0 all-gather.3.cloned.1.call-start
  9.9 258.4 %reduce-scatter.3.cloned.1.call-done = f32[32,128]{1,0:T(8,128)} async-done(((f32[4096,128]{1,0:T(8,128)}), f32[32,128]{1,0:T(8,128)}) %reduce-scatter.3.cloned.1.call-update) | async-done | bytes 16400 | tf_op jit(solution)/shard_map/reduce_scatter | solution.py:34
  268.3 0.0 all-gather.3.cloned.1.call-update
  268.3 0.0 reduce-scatter.5.cloned.1.call-start
  268.4 0.0 copy-done.4
  268.4 0.1 select_reduce_fusion
  268.6 1.3 multiply_reduce_fusion
  269.9 113.3 %psum.7 = f32[]{:T(128)} all-reduce(f32[]{:T(128)} %multiply_reduce_fusion), channel_id=1, replica_groups=mesh['dp'=128,'layer'=4] {'dp','layer'}, use_global_device_ids=true, to_apply=%region_4.5 | all-reduce | flops 1 | bytes 8 | tf_op jit(solution)/shard_map/psum | solution.py:36
  383.9 0.0 copy-start
  384.0 0.0 copy-start.1
  384.0 0.0 copy-start.2
  384.0 36.3 %all-gather.3.cloned.1.call-done = f32[4096,128]{1,0:T(8,128)} async-done(((f32[32,128]{1,0:T(8,128)}), f32[4096,128]{1,0:T(8,128)}) %all-gather.3.cloned.1.call-update) | async-done | bytes 2097168 | tf_op jit(solution)/shard_map/all_gather | solution.py:35
  420.3 2.3 reshape_reshape.3
  422.6 0.6 gather_fusion
  423.2 0.3 fusion.9
  423.5 2.7 gather_fusion.1
  426.2 2.0 convert_select_fusion
  428.2 2.7 select_n.93
  430.9 0.0 reduce-scatter.5.cloned.1.call-update
  430.9 0.0 all-gather.5.cloned.1.call-start
  431.0 246.3 %reduce-scatter.5.cloned.1.call-done = f32[32,128]{1,0:T(8,128)} async-done(((f32[4096,128]{1,0:T(8,128)}), f32[32,128]{1,0:T(8,128)}) %reduce-scatter.5.cloned.1.call-update) | async-done | bytes 16400 | tf_op jit(solution)/shard_map/reduce_scatter | solution.py:59
  677.2 1.3 convert_element_type.22
  678.6 0.0 all-gather.5.cloned.1.call-update
  678.6 0.1 fusion.11
  678.7 1.0 broadcast_select_fusion.1
  679.7 140.7 %all-gather.5.cloned.1.call-done = bf16[4096,128]{1,0:T(8,128)(2,1)} async-done(((bf16[32,128]{1,0:T(8,128)(2,1)}), bf16[4096,128]{1,0:T(8,128)(2,1)}) %all-gather.5.cloned.1.call-update) | async-done | bytes 1048592 | tf_op jit(solution)/shard_map/all_gather | solution.py:62
  820.3 2.3 broadcast_in_dim_reshape.3
  (11 shorter events, 0.1 us)
Async XLA Ops:
  7.2 261.2 %copy-start.4 = (s32[1,128]{1,0:T(1,128)S(1)}, s32[1,128]{1,0:T(1,128)}, u32[]{:S(2)}) copy-start(s32[1,128]{1,0:T(1,128)} %param.11) | copy-start | bytes 1540
  7.2 261.2 %copy-start.3 = (s32[1,128]{1,0:T(1,128)S(1)}, s32[1,128]{1,0:T(1,128)}, u32[]{:S(2)}) copy-start(s32[1,128]{1,0:T(1,128)} %param.10) | copy-start | bytes 1540
  7.2 261.1 %reduce-scatter.3.cloned.1.call-start = ((), (), s32[]{:S(2)}) async-start(), calls=%async_computation.2 | async-start | bytes 2113536 | tf_op jit(solution)/shard_map/reduce_scatter | solution.py:34
  9.9 410.4 %all-gather.3.cloned.1.call-start = ((), (), s32[]{:S(2)}) async-start(), calls=%async_computation.3 | async-start | bytes 2113536 | tf_op jit(solution)/shard_map/all_gather | solution.py:35
  268.3 408.9 %reduce-scatter.5.cloned.1.call-start = ((), (), s32[]{:S(2)}) async-start(), calls=%async_computation.4 | async-start | bytes 2113536 | tf_op jit(solution)/shard_map/reduce_scatter | solution.py:59
  383.9 39.3 %copy-start = (f32[1,3,2,2048]{3,2,1,0:T(2,128)S(1)}, f32[1,3,2,2048]{3,2,1,0:T(2,128)}, u32[]{:S(2)}) copy-start(f32[1,3,2,2048]{3,2,1,0:T(2,128)} %param.9) | copy-start | bytes 147460
  384.0 39.3 %copy-start.1 = (f32[1,3,2,2048]{3,2,1,0:T(2,128)S(1)}, f32[1,3,2,2048]{3,2,1,0:T(2,128)}, u32[]{:S(2)}) copy-start(f32[1,3,2,2048]{3,2,1,0:T(2,128)} %param.7) | copy-start | bytes 147460
  384.0 39.3 %copy-start.2 = (f32[1,3,2,2048]{3,2,1,0:T(2,128)S(1)}, f32[1,3,2,2048]{3,2,1,0:T(2,128)}, u32[]{:S(2)}) copy-start(f32[1,3,2,2048]{3,2,1,0:T(2,128)} %param.8) | copy-start | bytes 147460
  430.9 389.4 %all-gather.5.cloned.1.call-start = ((), (), s32[]{:S(2)}) async-start(), calls=%async_computation.5 | async-start | bytes 1056768 | tf_op jit(solution)/shard_map/all_gather | solution.py:62
Sparse Core Ops, SparseCore 0:
  12.6 255.6 reduce-scatter.2
  271.4 148.7 all-gather.2
  431.1 246.1 reduce-scatter.4
  680.6 139.6 all-gather.4
where the time goes:
time: 831 us; the launch traced here: 830 us
  waiting for transfers between devices  682 us (82%)
  blocking collectives  113 us (14%)
  between operations  15.8 us (2%)
  local copies, waits for them, and re-layouts  13.3 us (2%)
    reduce_scatter x1, waiting for transfers between devices, shards(): lax.psum_scatter(flat_grad, 'dp', scatter_dimension=0, tiled=True)  258 us
    reduce_scatter x1, waiting for transfers between devices, shards(): lax.psum_scatter(placed, 'dp', scatter_dimension=0, tiled=True)  246 us
    all_gather x1, waiting for transfers between devices, shards(): lax.all_gather(weight_share, 'dp', axis=0, tiled=True)  141 us
    psum x1, blocking collectives, shards(): squares = lax.psum(jnp.sum(grad_share * grad_share), ('dp', 'layer'))  113 us
    all_gather x1, waiting for transfers between devices, shards(): lax.all_gather(grad_share, 'dp', axis=0, tiled=True)  36.3 us
  transfers between devices with their start and end apart: 4, of which 4 were waited for; matrix products, arithmetic and copies ran while one was open for 0% of the time, Pallas kernels for 0%

commit v1 on v0

--- a/solution.py
+++ b/solution.py
@@ -59,9 +59,9 @@
     weight_share = lax.psum_scatter(placed, "dp", scatter_dimension=0, tiled=True).astype(
         jnp.bfloat16
     )
-    weights = lax.all_gather(weight_share, "dp", axis=0, tiled=True).reshape(
-        row_count, feature_count
-    )
+    weights = jnp.concatenate(
+        lax.all_to_all(jnp.stack([weight_share] * lax.axis_size("dp")), "dp", 0, 0), axis=0
+    ).reshape(row_count, feature_count)
     return (new_master[None], new_first[None], new_second[None], weights[None], grad_rms)
 
 

time: 831 us -> 767 us (0.923)
  waiting for transfers between devices: 682 us -> 592 us
  starting transfers between devices: 0.16 us -> 24.1 us
    all_gather x1 -> x0, waiting for transfers between devices: 141 us -> none  [shards(): lax.all_gather(weight_share, 'dp', axis=0, tiled=True)]
    all_to_all x0 -> x1, waiting for transfers between devices: none -> 50.8 us  [shards(): lax.all_to_all(jnp.stack([weight_share] * lax.axis_size('dp')), 'dp', 0, 0)]
    all_to_all x0 -> x1, starting transfers between devices: none -> 24 us  [shards(): lax.all_to_all(jnp.stack([weight_share] * lax.axis_size('dp')), 'dp', 0, 0)]
where the time goes in v1:
time: 767 us; the launch traced here: 764 us
  waiting for transfers between devices  592 us (77%)
  blocking collectives  113 us (15%)
  starting transfers between devices  24.1 us (3%)
  between operations  15.8 us (2%)
  local copies, waits for them, and re-layouts  13.3 us (2%)
    reduce_scatter x1, waiting for transfers between devices, shards(): lax.psum_scatter(flat_grad, 'dp', scatter_dimension=0, tiled=True)  258 us
    reduce_scatter x1, waiting for transfers between devices, shards(): lax.psum_scatter(placed, 'dp', scatter_dimension=0, tiled=True)  246 us
    psum x1, blocking collectives, shards(): squares = lax.psum(jnp.sum(grad_share * grad_share), ('dp', 'layer'))  113 us
    all_to_all x1, waiting for transfers between devices, shards(): lax.all_to_all(jnp.stack([weight_share] * lax.axis_size('dp')), 'dp', 0, 0)  50.8 us
    all_gather x1, waiting for transfers between devices, shards(): lax.all_gather(grad_share, 'dp', axis=0, tiled=True)  36.3 us
    all_to_all x1, starting transfers between devices, shards(): lax.all_to_all(jnp.stack([weight_share] * lax.axis_size('dp')), 'dp', 0, 0)  24 us
  transfers between devices with their start and end apart: 4, of which 4 were waited for; matrix products, arithmetic and copies ran while one was open for 0% of the time, Pallas kernels for 0%

profile of v1, /device:TPU:1, one launch (start us, length us, event | category | flops | bytes accessed | tf_op | source)
XLA Modules:
  0.0 763.8 jit_solution(6322918874845406969)
XLA Ops:
  7.2 0.0 copy-start.4
  7.2 0.0 copy-start.3
  7.2 0.0 reduce-scatter.3.cloned.1.call-start
  7.2 2.6 reshape.113
  9.8 0.0 reduce-scatter.3.cloned.1.call-update
  9.9 0.0 all-gather.2.cloned.1.call-start
  9.9 258.4 %reduce-scatter.3.cloned.1.call-done = f32[32,128]{1,0:T(8,128)} async-done(((f32[4096,128]{1,0:T(8,128)}), f32[32,128]{1,0:T(8,128)}) %reduce-scatter.3.cloned.1.call-update) | async-done | bytes 16400 | tf_op jit(solution)/shard_map/reduce_scatter | solution.py:34
  268.3 0.0 all-gather.2.cloned.1.call-update
  268.3 0.0 reduce-scatter.5.cloned.1.call-start
  268.4 0.0 copy-done.4
  268.4 0.1 select_reduce_fusion
  268.6 1.3 multiply_reduce_fusion
  269.9 113.3 %psum.7 = f32[]{:T(128)} all-reduce(f32[]{:T(128)} %multiply_reduce_fusion), channel_id=1, replica_groups=mesh['dp'=128,'layer'=4] {'dp','layer'}, use_global_device_ids=true, to_apply=%region_4.5 | all-reduce | flops 1 | bytes 8 | tf_op jit(solution)/shard_map/psum | solution.py:36
  383.9 0.0 copy-start
  383.9 0.0 copy-start.1
  384.0 0.0 copy-start.2
  384.0 36.3 %all-gather.2.cloned.1.call-done = f32[4096,128]{1,0:T(8,128)} async-done(((f32[32,128]{1,0:T(8,128)}), f32[4096,128]{1,0:T(8,128)}) %all-gather.2.cloned.1.call-update) | async-done | bytes 2097168 | tf_op jit(solution)/shard_map/all_gather | solution.py:35
  420.3 2.3 reshape_reshape.3
  422.6 0.6 gather_fusion
  423.2 0.3 fusion.9
  423.5 2.7 gather_fusion.1
  426.2 2.0 convert_select_fusion
  428.2 2.7 select_n.93
  430.9 0.0 reduce-scatter.5.cloned.1.call-update
  430.9 246.3 %reduce-scatter.5.cloned.1.call-done = f32[32,128]{1,0:T(8,128)} async-done(((f32[4096,128]{1,0:T(8,128)}), f32[32,128]{1,0:T(8,128)}) %reduce-scatter.5.cloned.1.call-update) | async-done | bytes 16400 | tf_op jit(solution)/shard_map/reduce_scatter | solution.py:59
  677.2 0.7 convert_element_type.22
  677.9 1.1 stack.2
  679.0 24.0 %all-to-all-start = ((bf16[128,32,128]{2,1,0:T(8,128)(2,1)}), bf16[128,32,128]{2,1,0:T(8,128)(2,1)S(1)}, u32[]{:S(2)}, u32[]{:S(2)}) async-start(bf16[128,32,128]{2,1,0:T(8,128)(2,1)} %stack.2), calls=%async_computation.2 | async-start | bytes 2097152 | tf_op jit(solution)/shard_map/all_to_all | solution.py:63
  703.1 0.1 fusion.11
  703.2 1.0 broadcast_select_fusion.1
  704.1 50.8 %all-to-all-done = bf16[128,32,128]{2,1,0:T(8,128)(2,1)S(1)} async-done(((bf16[128,32,128]{2,1,0:T(8,128)(2,1)}), bf16[128,32,128]{2,1,0:T(8,128)(2,1)S(1)}, u32[]{:S(2)}, u32[]{:S(2)}) %all-to-all-start) | async-done | bytes 1048608 | tf_op jit(solution)/shard_map/all_to_all | solution.py:63
  754.9 1.3 broadcast_in_dim_reshape_reshape.3
  (11 shorter events, 0.1 us)
Async XLA Ops:
  7.2 261.2 %copy-start.4 = (s32[1,128]{1,0:T(1,128)S(1)}, s32[1,128]{1,0:T(1,128)}, u32[]{:S(2)}) copy-start(s32[1,128]{1,0:T(1,128)} %param.11) | copy-start | bytes 1540
  7.2 261.2 %copy-start.3 = (s32[1,128]{1,0:T(1,128)S(1)}, s32[1,128]{1,0:T(1,128)}, u32[]{:S(2)}) copy-start(s32[1,128]{1,0:T(1,128)} %param.10) | copy-start | bytes 1540
  7.2 261.1 %reduce-scatter.3.cloned.1.call-start = ((), (), s32[]{:S(2)}) async-start(), calls=%async_computation.3 | async-start | bytes 2113536 | tf_op jit(solution)/shard_map/reduce_scatter | solution.py:34
  9.9 410.4 %all-gather.2.cloned.1.call-start = ((), (), s32[]{:S(2)}) async-start(), calls=%async_computation.4 | async-start | bytes 2113536 | tf_op jit(solution)/shard_map/all_gather | solution.py:35
  268.3 408.9 %reduce-scatter.5.cloned.1.call-start = ((), (), s32[]{:S(2)}) async-start(), calls=%async_computation.5 | async-start | bytes 2113536 | tf_op jit(solution)/shard_map/reduce_scatter | solution.py:59
  383.9 39.3 %copy-start = (f32[1,3,2,2048]{3,2,1,0:T(2,128)S(1)}, f32[1,3,2,2048]{3,2,1,0:T(2,128)}, u32[]{:S(2)}) copy-start(f32[1,3,2,2048]{3,2,1,0:T(2,128)} %param.9) | copy-start | bytes 147460
  383.9 39.3 %copy-start.1 = (f32[1,3,2,2048]{3,2,1,0:T(2,128)S(1)}, f32[1,3,2,2048]{3,2,1,0:T(2,128)}, u32[]{:S(2)}) copy-start(f32[1,3,2,2048]{3,2,1,0:T(2,128)} %param.7) | copy-start | bytes 147460
  384.0 39.3 %copy-start.2 = (f32[1,3,2,2048]{3,2,1,0:T(2,128)S(1)}, f32[1,3,2,2048]{3,2,1,0:T(2,128)}, u32[]{:S(2)}) copy-start(f32[1,3,2,2048]{3,2,1,0:T(2,128)} %param.8) | copy-start | bytes 147460
  679.0 75.9 %all-to-all-start = ((bf16[128,32,128]{2,1,0:T(8,128)(2,1)}), bf16[128,32,128]{2,1,0:T(8,128)(2,1)S(1)}, u32[]{:S(2)}, u32[]{:S(2)}) async-start(bf16[128,32,128]{2,1,0:T(8,128)(2,1)} %stack.2), calls=%async_computation.2 | async-start | bytes 2097152 | tf_op jit(solution)/shard_map/all_to_all | solution.py:63
Sparse Core Ops, SparseCore 0:
  12.6 255.6 reduce-scatter.2
  271.4 148.7 all-gather.1
  431.1 246.0 reduce-scatter.4
